TPU v7x, 32 devices: a whole 2x2x4 slice. The times are simulated.
32 devices in a mesh: gx: 4 (over y, x), gy: 8 (over z, core).
Axes of the slice: x: 2, y: 2, z: 4, core: 2. Of those that a mesh axis runs over, the one named last changes fastest.
Arguments:
- thermal_field: bfloat16 [384, 384, 128], P('gx', 'gy'), may hold values from -6 to 6
- probe_range_east: bfloat16 [384, 128], P('gx'), may hold values from -0.3125 to 0.3125
- probe_range_north: bfloat16 [384, 128], P('gy'), may hold values from -0.3125 to 0.3125
- probe_range_upward: bfloat16 [128, 128], replicated, may hold values from -0.5 to 0.5
- gauss_kernel_east: bfloat16 [384, 384], replicated, may hold values from -0.3125 to 0.3125
- gauss_kernel_north: bfloat16 [384, 384], replicated, may hold values from -0.3125 to 0.3125
- gauss_kernel_upward: bfloat16 [384, 128], replicated, may hold values from -0.5 to 0.5
Outputs:
- factor_x: float32 [384, 128], P('gx')
- factor_y: float32 [384, 128], P('gy')
- factor_z: float32 [128, 128], replicated
- core_sketch: float32 [384, 384, 384], P('gx', None, 'gy')
All inputs are finite; a program needn't handle non-finite values.
Results may differ from a plain program's by a relative error of at most 0.0029.
Values may be sent and summed in bfloat16 or wider, within the bound.
A program may use at most 64 MiB of HBM per device.

v0:
```python
import jax
import jax.numpy as jnp
from jax import lax
from jax.sharding import PartitionSpec as P


def per_device(
    thermal_field,
    probe_range_east,
    probe_range_north,
    probe_range_upward,
    gauss_kernel_east,
    gauss_kernel_north,
    gauss_kernel_upward,
):
    highest = lax.Precision.HIGHEST
    line_tally, span_breadth, height_tally = thermal_field.shape
    width = probe_range_upward.shape[1]
    unrolled_tensor = thermal_field.reshape(line_tally * span_breadth, height_tally)
    weighted = jnp.dot(
        unrolled_tensor, probe_range_upward, preferred_element_type=jnp.float32
    ).reshape(line_tally, span_breadth, width)
    along_x = probe_range_east.astype(jnp.float32)
    along_y = probe_range_north.astype(jnp.float32)
    part_x = jnp.sum(weighted * along_y[None, :, :], axis=1)
    part_y = jnp.sum(weighted * along_x[:, None, :], axis=0)
    khatri = (
        (along_x[:, None, :] * along_y[None, :, :])
        .astype(jnp.bfloat16)
        .reshape(line_tally * span_breadth, width)
    )
    part_z = lax.dot_general(
        unrolled_tensor, khatri, (((0,), (0,)), ((), ())), preferred_element_type=jnp.float32
    )
    factor_x = lax.psum(part_x, "gy")
    factor_y = lax.psum(part_y, "gx")
    factor_z = lax.psum(part_z, ("gx", "gy"))
    mixer_zf = gauss_kernel_upward.astype(jnp.float32)
    mixer_yf = gauss_kernel_north.astype(jnp.float32)
    mixed = jnp.einsum(
        "ijl,ai->ajl",
        lax.all_to_all(thermal_field, "gx", split_axis=2, concat_axis=0, tiled=True),
        gauss_kernel_east,
        preferred_element_type=jnp.float32,
    )
    mixed = jnp.einsum(
        "ajl,cl->ajc",
        lax.all_to_all(mixed, "gx", split_axis=0, concat_axis=2, tiled=True),
        mixer_zf,
        precision=highest,
    )
    core_sketch = jnp.einsum(
        "ajc,bj->abc",
        lax.all_to_all(mixed, "gy", split_axis=2, concat_axis=1, tiled=True),
        mixer_yf,
        precision=highest,
    )
    return (factor_x, factor_y, factor_z, core_sketch)


def solution(mesh):
    in_specs = (P("gx", "gy", None), P("gx", None), P("gy", None), P(), P(), P(), P())
    out_specs = (P("gx", None), P("gy", None), P(), P("gx", None, "gy"))
    return jax.shard_map(
        per_device, mesh=mesh, in_specs=in_specs, out_specs=out_specs, check_vma=False
    )
```

profile of v0, /device:TPU:1, one launch (start us, length us, event | category | flops | bytes accessed | tf_op | source)
XLA Modules:
  0.0 388.5 jit_solution(121109077919172618)
XLA Ops:
  7.2 0.0 copy-start
  7.2 2.4 copy.38
  9.6 22.6 %all_to_all.54 = bf16[96,48,128]{0,1,2:T(8,128)(2,1)S(1)} all-to-all(bf16[96,48,128]{0,1,2:T(8,128)(2,1)S(1)} %copy.38), channel_id=1, replica_groups=mesh['gx'=4,'gy'=8] {'gx'}, dimensions={2} | all-to-all | bytes 2359296 | tf_op jit(solution)/shard_map/all_to_all | solution.py:42
  32.2 1.2 copy.40
  33.4 1.9 all_to_all.42
  35.3 0.0 copy-done.2
  35.3 2.2 fusion.5
  37.5 6.0 %copy.41 = f32[384,48,32]{1,2,0:T(8,128)} copy(f32[384,48,32]{0,1,2:T(8,128)S(1)} %fusion.5) | data formatting | bytes 4718592 | tf_op jit(solution)/shard_map/ijl,ai->ajl/dot_general | solution.py:40
  43.5 8.2 %reshape.20 = f32[4,1,147456]{2,1,0:T(1,128)} reshape(f32[384,32,48]{2,1,0:T(8,128)} %bitcast.42) | data formatting | bytes 4718592
  51.7 29.2 %all_to_all.55 = f32[4,1,147456]{2,1,0:T(1,128)S(1)} all-to-all(f32[4,1,147456]{2,1,0:T(1,128)} %reshape.20), channel_id=1, replica_groups=mesh['gx'=4,'gy'=8] {'gx'}, dimensions={0} | all-to-all | bytes 4718592 | tf_op jit(solution)/shard_map/all_to_all | solution.py:48
  80.9 0.5 broadcast.2
  81.4 8.3 %reduce = f32[4,147456]{1,0:T(4,128)} reduce(f32[4,1,147456]{2,1,0:T(1,128)S(1)} %all_to_all.55, f32[]{:T(128)} %broadcast.2), dimensions={1}, to_apply=%all_to_all.43.reduce_sub_computation | reduce | bytes 4718596 | tf_op jit(solution)/shard_map/all_to_all | solution.py:48
  89.7 7.3 %reshape.21 = f32[384,32,48]{2,1,0:T(8,128)} reshape(f32[4,147456]{1,0:T(4,128)} %reduce) | data formatting | bytes 4718592
  96.9 6.2 %copy.42 = f32[4,96,48,32]{1,3,0,2:T(8,128)S(1)} copy(f32[4,96,48,32]{2,3,1,0:T(8,128)} %bitcast.41) | data formatting | bytes 4718592 | tf_op jit(solution)/shard_map/all_to_all | solution.py:48
  103.1 0.0 copy-done.3
  103.1 7.1 %fusion.7 = f32[96,48,384]{2,0,1:T(8,128)} fusion(f32[96,48,128]{0,2,1:T(8,128)S(1)} %bitcast.43, bf16[384,128]{1,0:T(8,128)(2,1)S(1)} %copy-done.3), kind=kOutput, calls=%fused_computation.11 | convolution fusion | flops 2717908992 | bytes 9535488 | tf_op jit(solution)/shard_map/ajl,cl->ajc/dot_general | solution.py:46
  110.2 9.0 %copy.44 = f32[96,48,384]{0,1,2:T(8,128)} copy(f32[96,48,384]{2,0,1:T(8,128)} %fusion.7) | data formatting | bytes 14155776 | tf_op jit(solution)/shard_map/ajl,cl->ajc/dot_general | solution.py:46
  119.2 8.6 %all-to-all-start.2 = ((f32[96,48,384]{0,1,2:T(8,128)}), f32[96,48,384]{0,1,2:T(8,128)}, u32[]{:S(2)}, u32[]{:S(2)}) async-start(f32[96,48,384]{0,1,2:T(8,128)} %copy.44), calls=%async_computation.2 | async-start | bytes 18874368 | tf_op jit(solution)/shard_map/all_to_all | solution.py:54
  127.8 0.0 all-reduce.2.cloned.1.call-start
  127.8 0.0 copy-done.5
  127.8 0.0 copy-done.4
  127.9 1.1 fusion.3
  129.0 0.0 all-reduce.2.cloned.1.call-update
  129.0 0.5 multiply_reduce_fusion
  129.6 13.2 %psum.22 = f32[48,128]{1,0:T(8,128)} all-reduce(f32[48,128]{1,0:T(8,128)S(1)} %get-tuple-element.20), channel_id=1, replica_groups=mesh['gx'=4,'gy'=8] {'gx'}, use_global_device_ids=true, to_apply=%region_3.0 | all-reduce | flops 6144 | bytes 49152 | tf_op jit(solution)/shard_map/psum | solution.py:36
  142.8 207.4 %psum.21 = f32[96,128]{1,0:T(8,128)} all-reduce(f32[96,128]{1,0:T(8,128)S(1)} %get-tuple-element.21), channel_id=1, replica_groups=mesh['gx'=4,'gy'=8] {'gy'}, use_global_device_ids=true, to_apply=%region_1.0 | all-reduce | flops 12288 | bytes 98304 | tf_op jit(solution)/shard_map/psum | solution.py:35
  350.3 1.6 copy.48
  351.8 0.0 all-to-all-done.2
  351.8 10.1 %copy.46 = f32[96,8,48,48]{0,3,2,1:T(8,128)} copy(f32[96,8,48,48]{0,2,3,1:T(8,128)} %bitcast.13) | data formatting | bytes 14155776 | tf_op jit(solution)/shard_map/all_to_all | solution.py:54
  362.0 9.0 %copy.47 = f32[96,384,48]{1,2,0:T(8,128)} copy(f32[96,384,48]{0,2,1:T(8,128)} %bitcast.40) | data formatting | bytes 14155776 | tf_op jit(solution)/shard_map/all_to_all | solution.py:54
  371.0 0.0 copy-done
  371.0 10.7 %convolution_bitcast_fusion = f32[96,384,48]{1,2,0:T(8,128)} fusion(f32[96,384,48]{1,2,0:T(8,128)} %copy.47, bf16[384,384]{1,0:T(8,128)(2,1)S(1)} %copy-done), kind=kOutput, calls=%fused_computation | convolution fusion | flops 8153726976 | bytes 14450688 | tf_op jit(solution)/shard_map/ajc,bj->abc/dot_general | solution.py:52
  (11 shorter events, 0.0 us)
Async XLA Ops:
  7.2 363.8 %copy-start = (bf16[384,384]{1,0:T(8,128)(2,1)S(1)}, bf16[384,384]{1,0:T(8,128)(2,1)}, u32[]{:S(2)}) copy-start(bf16[384,384]{1,0:T(8,128)(2,1)} %param.12) | copy-start | bytes 884740
  32.2 3.1 copy-start.2
  96.9 6.2 %copy-start.3 = (bf16[384,128]{1,0:T(8,128)(2,1)S(1)}, bf16[384,128]{1,0:T(8,128)(2,1)}, u32[]{:S(2)}) copy-start(bf16[384,128]{1,0:T(8,128)(2,1)} %param.13) | copy-start | bytes 294916
  119.2 8.6 %copy-start.5 = (bf16[48,128]{1,0:T(8,128)(2,1)S(1)}, bf16[48,128]{1,0:T(8,128)(2,1)}, u32[]{:S(2)}) copy-start(bf16[48,128]{1,0:T(8,128)(2,1)} %param.9) | copy-start | bytes 36868
  119.2 8.6 %copy-start.4 = (bf16[96,128]{1,0:T(8,128)(2,1)S(1)}, bf16[96,128]{1,0:T(8,128)(2,1)}, u32[]{:S(2)}) copy-start(bf16[96,128]{1,0:T(8,128)(2,1)} %param.8) | copy-start | bytes 73732
  119.2 8.7 %copy-start.1 = (bf16[96,48,128]{2,1,0:T(8,128)(2,1)S(1)}, bf16[96,48,128]{2,1,0:T(8,128)(2,1)}, u32[]{:S(2)}) copy-start(bf16[96,48,128]{2,1,0:T(8,128)(2,1)} %param.7) | copy-start | bytes 3538948
  119.2 232.6 %all-to-all-start.2 = ((f32[96,48,384]{0,1,2:T(8,128)}), f32[96,48,384]{0,1,2:T(8,128)}, u32[]{:S(2)}, u32[]{:S(2)}) async-start(f32[96,48,384]{0,1,2:T(8,128)} %copy.44), calls=%async_computation.2 | async-start | bytes 18874368 | tf_op jit(solution)/shard_map/all_to_all | solution.py:54
  127.8 1.2 copy-start.6
  127.8 222.4 %all-reduce.2.cloned.1.call-start = ((), (), s32[]{:S(2)}) async-start(), calls=%async_computation.3 | async-start | bytes 131072 | tf_op jit(solution)/shard_map/psum | solution.py:37
Sparse Core Ops, SparseCore 0:
  134.8 161.1 all-reduce.1
where the time goes:
time: 391 us; the launch traced here: 389 us
  blocking collectives  272 us (70%)
  local copies, waits for them, and re-layouts  63.4 us (16%)
  matrix products  21.6 us (6%)
  between operations  14.1 us (4%)
  starting transfers between devices  8.62 us (2%)
  other arithmetic  8.29 us (2%)
    psum x1, blocking collectives, per_device(): factor_x = lax.psum(part_x, 'gy')  207 us
    all_to_all x1, blocking collectives, per_device(): lax.all_to_all(mixed, 'gx', split_axis=0, concat_axis=2, tiled=True)  29.2 us
    all_to_all x1, blocking collectives, per_device(): lax.all_to_all(thermal_field, 'gx', split_axis=2, concat_axis=0, tiled=True)  22.6 us
    unnamed x18, local copies, waits for them, and re-layouts  19.5 us
    all_to_all x2, local copies, waits for them, and re-layouts, per_device(): lax.all_to_all(mixed, 'gy', split_axis=2, concat_axis=1, tiled=True)  19.2 us
    psum x1, blocking collectives, per_device(): factor_y = lax.psum(part_y, 'gx')  13.2 us
    dot_general x1, matrix products, per_device(): jnp.einsum('ajc,bj->abc', lax.all_to_all(mixed, 'gy', split_axis=2, conca...  10.7 us
    dot_general x1, local copies, waits for them, and re-layouts, per_device(): jnp.einsum('ajl,cl->ajc', lax.all_to_all(mixed, 'gx', split_axis=0, conca...  8.98 us
  transfers between devices with their start and end apart: 2, of which 0 were waited for; matrix products, arithmetic and copies ran while one was open for 1% of the time, Pallas kernels for 0%

commit v1 on v0

--- a/solution.py
+++ b/solution.py
@@ -13,7 +13,6 @@
     gauss_kernel_north,
     gauss_kernel_upward,
 ):
-    highest = lax.Precision.HIGHEST
     line_tally, span_breadth, height_tally = thermal_field.shape
     width = probe_range_upward.shape[1]
     unrolled_tensor = thermal_field.reshape(line_tally * span_breadth, height_tally)
@@ -35,25 +34,24 @@
     factor_x = lax.psum(part_x, "gy")
     factor_y = lax.psum(part_y, "gx")
     factor_z = lax.psum(part_z, ("gx", "gy"))
-    mixer_zf = gauss_kernel_upward.astype(jnp.float32)
-    mixer_yf = gauss_kernel_north.astype(jnp.float32)
+    bf = jnp.bfloat16
     mixed = jnp.einsum(
         "ijl,ai->ajl",
         lax.all_to_all(thermal_field, "gx", split_axis=2, concat_axis=0, tiled=True),
         gauss_kernel_east,
         preferred_element_type=jnp.float32,
-    )
+    ).astype(bf)
     mixed = jnp.einsum(
         "ajl,cl->ajc",
         lax.all_to_all(mixed, "gx", split_axis=0, concat_axis=2, tiled=True),
-        mixer_zf,
-        precision=highest,
-    )
+        gauss_kernel_upward,
+        preferred_element_type=jnp.float32,
+    ).astype(bf)
     core_sketch = jnp.einsum(
         "ajc,bj->abc",
         lax.all_to_all(mixed, "gy", split_axis=2, concat_axis=1, tiled=True),
-        mixer_yf,
-        precision=highest,
+        gauss_kernel_north,
+        preferred_element_type=jnp.float32,
     )
     return (factor_x, factor_y, factor_z, core_sketch)
 

time: 391 us -> 265 us (0.68)
  blocking collectives: 272 us -> 159 us
  waiting for transfers between devices: 0.02 us -> 19.7 us
  local copies, waits for them, and re-layouts: 63.4 us -> 49.3 us
  other arithmetic: 8.29 us -> 0.01 us
  matrix products: 21.6 us -> 13.7 us
    psum x1, blocking collectives: 207 us -> 106 us  [per_device(): factor_x = lax.psum(part_x, 'gy')]
    psum x1, waiting for transfers between devices: 0.01 us -> 19.6 us  [per_device(): factor_z = lax.psum(part_z, ('gx', 'gy'))]
    dot_general x2 -> x0, local copies, waits for them, and re-layouts: 15 us -> none  [the longest x1 8.98 us: per_device(): jnp.einsum('ajl,cl->ajc', lax.all_to_all(mixed, 'gx', split_axis=0, conca...]
    convert_element_type x0 -> x2, local copies, waits for them, and re-layouts: none -> 12.3 us  [the longest x1 7.02 us: per_device(): mixed = jnp.einsum('ajl,cl->ajc', lax.all_to_all(mixed, 'gx', split_axis=...]
    all_to_all x1, blocking collectives: 29.2 us -> 17.3 us  [per_device(): lax.all_to_all(mixed, 'gx', split_axis=0, concat_axis=2, tiled=True)]
    all_to_all x1 -> x0, other arithmetic: 8.28 us -> none  [per_device(): lax.all_to_all(mixed, 'gx', split_axis=0, concat_axis=2, tiled=True)]
    all_to_all x2, local copies, waits for them, and re-layouts: 19.2 us -> 13.1 us  [per_device(): lax.all_to_all(mixed, 'gy', split_axis=2, concat_axis=1, tiled=True)]
    unnamed x18, local copies, waits for them, and re-layouts: 19.5 us -> 14.2 us
  transfers between devices with their start and end apart: 2 -> 2, of which waited for: 0 -> 1; matrix products, arithmetic and copies ran while one was open for 1% -> 1% of each run, Pallas kernels for 0% -> 0%
where the time goes in v1:
time: 265 us; the launch traced here: 264 us
  blocking collectives  159 us (60%)
  local copies, waits for them, and re-layouts  49.3 us (19%)
  waiting for transfers between devices  19.7 us (7%)
  between operations  14.2 us (5%)
  matrix products  13.7 us (5%)
  starting transfers between devices  8.58 us (3%)
    psum x1, blocking collectives, per_device(): factor_x = lax.psum(part_x, 'gy')  106 us
    all_to_all x1, blocking collectives, per_device(): lax.all_to_all(thermal_field, 'gx', split_axis=2, concat_axis=0, tiled=True)  22.6 us
    psum x1, waiting for transfers between devices, per_device(): factor_z = lax.psum(part_z, ('gx', 'gy'))  19.6 us
    all_to_all x1, blocking collectives, per_device(): lax.all_to_all(mixed, 'gx', split_axis=0, concat_axis=2, tiled=True)  17.3 us
    unnamed x18, local copies, waits for them, and re-layouts  14.2 us
    psum x1, blocking collectives, per_device(): factor_y = lax.psum(part_y, 'gx')  13.2 us
    all_to_all x2, local copies, waits for them, and re-layouts, per_device(): lax.all_to_all(mixed, 'gy', split_axis=2, concat_axis=1, tiled=True)  13.1 us
    all_to_all x1, starting transfers between devices, per_device(): lax.all_to_all(mixed, 'gy', split_axis=2, concat_axis=1, tiled=True)  8.58 us
  transfers between devices with their start and end apart: 2, of which 1 were waited for; matrix products, arithmetic and copies ran while one was open for 1% of the time, Pallas kernels for 0%

profile of v1, /device:TPU:1, one launch (start us, length us, event | category | flops | bytes accessed | tf_op | source)
XLA Modules:
  0.0 264.4 jit_solution(4914472566553190017)
XLA Ops:
  7.2 0.0 copy-start
  7.2 2.4 copy.38
  9.6 22.6 %all_to_all.54 = bf16[96,48,128]{0,1,2:T(8,128)(2,1)S(1)} all-to-all(bf16[96,48,128]{0,1,2:T(8,128)(2,1)S(1)} %copy.38), channel_id=1, replica_groups=mesh['gx'=4,'gy'=8] {'gx'}, dimensions={2} | all-to-all | bytes 2359296 | tf_op jit(solution)/shard_map/all_to_all | solution.py:40
  32.2 1.2 copy.40
  33.4 0.0 copy-start.2
  33.4 1.1 all_to_all.42
  34.5 0.0 copy-done.2
  34.5 1.9 convolution_convert_fusion.1
  36.4 5.3 %copy.41 = bf16[384,48,32]{1,2,0:T(8,128)(2,1)S(1)} copy(bf16[384,48,32]{0,1,2:T(8,128)(2,1)} %convolution_convert_fusion.1) | data formatting | bytes 2359296 | tf_op jit(solution)/shard_map/convert_element_type | solution.py:43
  41.7 6.0 %reshape.20 = bf16[4,2,73728]{2,1,0:T(2,128)(2,1)} reshape(bf16[384,32,48]{2,1,0:T(8,128)(2,1)S(1)} %bitcast.42) | data formatting | bytes 2359296
  47.8 17.3 %all_to_all.55 = bf16[4,2,73728]{2,1,0:T(2,128)(2,1)} all-to-all(bf16[4,2,73728]{2,1,0:T(2,128)(2,1)} %reshape.20), channel_id=1, replica_groups=mesh['gx'=4,'gy'=8] {'gx'}, dimensions={0} | all-to-all | bytes 2359296 | tf_op jit(solution)/shard_map/all_to_all | solution.py:46
  65.0 4.2 %reshape.21 = bf16[384,32,48]{2,1,0:T(8,128)(2,1)S(1)} reshape(bf16[4,2,73728]{2,1,0:T(2,128)(2,1)} %all_to_all.55) | data formatting | bytes 2359296
  69.2 5.4 %copy.42 = bf16[4,96,48,32]{1,3,0,2:T(8,128)(2,1)} copy(bf16[4,96,48,32]{2,3,1,0:T(8,128)(2,1)S(1)} %bitcast.41) | data formatting | bytes 2359296 | tf_op jit(solution)/shard_map/all_to_all | solution.py:46
  74.6 1.9 copy.43
  76.6 0.0 copy-done.3
  76.6 2.8 %convolution_convert_fusion = bf16[96,48,384]{2,1,0:T(8,128)(2,1)} fusion(bf16[96,48,128]{2,1,0:T(8,128)(2,1)S(1)} %copy.43, bf16[384,128]{1,0:T(8,128)(2,1)S(1)} %copy-done.3), kind=kOutput, calls=%fused_computation.1 | convolution fusion | flops 454754304 | bytes 4816896 | tf_op jit(solution)/shard_map/ajl,cl->ajc/dot_general | solution.py:44
  79.4 7.0 %copy.44 = bf16[96,48,384]{0,1,2:T(8,128)(2,1)} copy(bf16[96,48,384]{2,1,0:T(8,128)(2,1)} %convolution_convert_fusion) | data formatting | bytes 7077888 | tf_op jit(solution)/shard_map/convert_element_type | solution.py:49
  86.5 8.6 %all-to-all-start.2 = ((bf16[96,48,384]{0,1,2:T(8,128)(2,1)}), bf16[96,48,384]{0,1,2:T(8,128)(2,1)}, u32[]{:S(2)}, u32[]{:S(2)}) async-start(bf16[96,48,384]{0,1,2:T(8,128)(2,1)} %copy.44), calls=%async_computation.2 | async-start | bytes 9437184 | tf_op jit(solution)/shard_map/all_to_all | solution.py:52
  95.1 0.0 all-reduce.2.cloned.1.call-start
  95.1 0.0 copy-done.5
  95.1 0.0 copy-done.4
  95.1 1.1 fusion.3
  96.3 0.0 all-reduce.2.cloned.1.call-update
  96.3 0.5 multiply_reduce_fusion
  96.8 13.2 %psum.22 = f32[48,128]{1,0:T(8,128)} all-reduce(f32[48,128]{1,0:T(8,128)S(1)} %get-tuple-element.20), channel_id=1, replica_groups=mesh['gx'=4,'gy'=8] {'gx'}, use_global_device_ids=true, to_apply=%region_3.0 | all-reduce | flops 6144 | bytes 49152 | tf_op jit(solution)/shard_map/psum | solution.py:35
  110.1 105.9 %psum.21 = f32[96,128]{1,0:T(8,128)} all-reduce(f32[96,128]{1,0:T(8,128)S(1)} %get-tuple-element.21), channel_id=1, replica_groups=mesh['gx'=4,'gy'=8] {'gy'}, use_global_device_ids=true, to_apply=%region_1.0 | all-reduce | flops 12288 | bytes 98304 | tf_op jit(solution)/shard_map/psum | solution.py:34
  216.0 19.6 %all-reduce.2.cloned.1.call-done = f32[128,128]{0,1:T(8,128)} async-done(((f32[128,128]{0,1:T(8,128)}), f32[128,128]{0,1:T(8,128)}) %all-reduce.2.cloned.1.call-update) | async-done | bytes 65552 | tf_op jit(solution)/shard_map/psum | solution.py:36
  235.6 1.6 copy.48
  237.2 0.0 all-to-all-done.2
  237.2 5.7 %copy.46 = bf16[96,8,48,48]{0,3,2,1:T(8,128)(2,1)} copy(bf16[96,8,48,48]{0,2,3,1:T(8,128)(2,1)} %bitcast.13) | data formatting | bytes 7077888 | tf_op jit(solution)/shard_map/all_to_all | solution.py:52
  242.9 7.3 %copy.47 = bf16[96,384,48]{1,2,0:T(8,128)(2,1)} copy(bf16[96,384,48]{0,2,1:T(8,128)(2,1)} %bitcast.40) | data formatting | bytes 7077888 | tf_op jit(solution)/shard_map/all_to_all | solution.py:52
  250.2 7.3 %convolution_bitcast_fusion = f32[96,384,48]{1,2,0:T(8,128)} fusion(bf16[96,384,48]{1,2,0:T(8,128)(2,1)} %copy.47, bf16[384,384]{1,0:T(8,128)(2,1)S(1)} %copy-done), kind=kOutput, calls=%fused_computation | convolution fusion | flops 1358954496 | bytes 10911744 | tf_op jit(solution)/shard_map/ajc,bj->abc/dot_general | solution.py:50
  (10 shorter events, 0.0 us)
Async XLA Ops:
  7.2 243.1 %copy-start = (bf16[384,384]{1,0:T(8,128)(2,1)S(1)}, bf16[384,384]{1,0:T(8,128)(2,1)}, u32[]{:S(2)}) copy-start(bf16[384,384]{1,0:T(8,128)(2,1)} %param.12) | copy-start | bytes 884740
  33.4 1.1 copy-start.2
  74.6 2.0 copy-start.3
  86.5 8.6 %copy-start.5 = (bf16[48,128]{1,0:T(8,128)(2,1)S(1)}, bf16[48,128]{1,0:T(8,128)(2,1)}, u32[]{:S(2)}) copy-start(bf16[48,128]{1,0:T(8,128)(2,1)} %param.9) | copy-start | bytes 36868
  86.5 8.6 %copy-start.4 = (bf16[96,128]{1,0:T(8,128)(2,1)S(1)}, bf16[96,128]{1,0:T(8,128)(2,1)}, u32[]{:S(2)}) copy-start(bf16[96,128]{1,0:T(8,128)(2,1)} %param.8) | copy-start | bytes 73732
  86.5 8.6 %copy-start.1 = (bf16[96,48,128]{2,1,0:T(8,128)(2,1)S(1)}, bf16[96,48,128]{2,1,0:T(8,128)(2,1)}, u32[]{:S(2)}) copy-start(bf16[96,48,128]{2,1,0:T(8,128)(2,1)} %param.7) | copy-start | bytes 3538948
  86.5 150.7 %all-to-all-start.2 = ((bf16[96,48,384]{0,1,2:T(8,128)(2,1)}), bf16[96,48,384]{0,1,2:T(8,128)(2,1)}, u32[]{:S(2)}, u32[]{:S(2)}) async-start(bf16[96,48,384]{0,1,2:T(8,128)(2,1)} %copy.44), calls=%async_computation.2 | async-start | bytes 9437184 | tf_op jit(solution)/shard_map/all_to_all | solution.py:52
  95.1 1.2 copy-start.6
  95.1 140.5 %all-reduce.2.cloned.1.call-start = ((), (), s32[]{:S(2)}) async-start(), calls=%async_computation.3 | async-start | bytes 131072 | tf_op jit(solution)/shard_map/psum | solution.py:36
Sparse Core Ops, SparseCore 0:
  102.0 133.5 all-reduce.1

commit v2 on v1

v2 whole, which is shorter than its diff:
```python
import functools

import jax
import jax.numpy as jnp
from jax import lax
from jax.experimental import pallas as pl
from jax.experimental.pallas import tpu as pltpu
from jax.sharding import PartitionSpec as P

MESH = pl.DeviceIdType.MESH
VMEM = pl.BlockSpec(memory_space=pltpu.VMEM)
ANY = pl.BlockSpec(memory_space=pl.ANY)
BF = jnp.bfloat16
F32 = jnp.float32


def remote(src, dst, send, recv, where):
    copy = pltpu.make_async_remote_copy(
        src_ref=src, dst_ref=dst, send_sem=send, recv_sem=recv, device_id=where, device_id_type=MESH
    )
    copy.start()
    return copy


def mix_x_kernel(n, chunks, t_ref, g_ref, w_ref, x_buf, y_buf, s1, r1, s2, r2, ls):
    gx, gy = lax.axis_index("gx"), lax.axis_index("gy")
    rows = t_ref.shape[0]
    a_rows = y_buf.shape[2]
    wide = t_ref.shape[1] // n
    part = wide // chunks
    barrier = pltpu.get_barrier_semaphore()
    for d in range(1, n):
        pl.semaphore_signal(barrier, inc=1, device_id=(lax.rem(gx + d, n), gy), device_id_type=MESH)
    pl.semaphore_wait(barrier, n - 1)

    first, second, local = [], [], []
    for m in range(chunks):
        for d in range(1, n):
            to = lax.rem(gx + d, n)
            lanes = pl.ds(pl.multiple_of(to * wide + m * part, 128), part)
            first.append(
                remote(t_ref.at[:, lanes], x_buf.at[m, gx], s1.at[m, d], r1.at[m, d], (to, gy))
            )
        lanes = pl.ds(pl.multiple_of(gx * wide + m * part, 128), part)
        own = pltpu.make_async_copy(t_ref.at[:, lanes], x_buf.at[m, gx], ls.at[m, 0])
        own.start()
        local.append(own)
    for m in range(chunks):
        local[m].wait()
        for d in range(1, n):
            first[m * (n - 1) + d - 1].wait()
        block = x_buf[m].reshape(n * rows, part)
        lanes = pl.ds(pl.multiple_of(gx * wide + m * part, 128), part)
        for d in range(1, n + 1):
            to = lax.rem(gx + d, n)
            y_buf[m, d - 1] = jnp.dot(g_ref[to], block, preferred_element_type=F32).astype(BF)
            if d < n:
                second.append(
                    remote(
                        y_buf.at[m, d - 1], w_ref.at[:, lanes], s2.at[m, d], r2.at[m, d], (to, gy)
                    )
                )
            else:
                own = pltpu.make_async_copy(y_buf.at[m, d - 1], w_ref.at[:, lanes], ls.at[m, 1])
                own.start()
                second.append(own)
    for copy in second:
        copy.wait()


def mix_x(field, gauss, n, a_rows):
    rows, lanes = field.shape
    wide = lanes // n
    chunks = 3 if wide % 384 == 0 else 1
    dma = lambda *shape: pltpu.SemaphoreType.DMA(shape)
    return pl.pallas_call(
        functools.partial(mix_x_kernel, n, chunks),
        out_shape=jax.ShapeDtypeStruct((a_rows, lanes), BF),
        in_specs=[VMEM, VMEM],
        out_specs=VMEM,
        scratch_shapes=[
            pltpu.VMEM((chunks, n, rows, wide // chunks), BF),
            pltpu.VMEM((chunks, n, a_rows, wide // chunks), BF),
            dma(chunks, n), dma(chunks, n), dma(chunks, n), dma(chunks, n), dma(chunks, 2),
        ],
        compiler_params=pltpu.CompilerParams(collective_id=0, has_side_effects=True),
    )(field, gauss)


def exchange_kernel(
    nx, ny, batches, per_c, w_ref, gt_ref, mask_ref, q_ref, py_ref,
    r_ref, qo_ref, pyo_ref,
    u_buf, q_in, q_all, y_in, z_in, z_own,
    us, ur, ul, qs, qr, ys, yr, zs, zr, gs, gr,
):
    gx, gy = lax.axis_index("gx"), lax.axis_index("gy")
    span = u_buf.shape[3]
    per = u_buf.shape[2]
    lanes = u_buf.shape[4]
    a_in = mask_ref.shape[0]
    deep = gt_ref.shape[1]
    x_rows = q_ref.shape[1] - z_in.shape[1]
    barrier = pltpu.get_barrier_semaphore()
    for d in range(1, ny):
        pl.semaphore_signal(barrier, inc=1, device_id=(gx, lax.rem(gy + d, ny)), device_id_type=MESH)
    for d in range(1, nx):
        pl.semaphore_signal(barrier, inc=1, device_id=(lax.rem(gx + d, nx), gy), device_id_type=MESH)
    pl.semaphore_wait(barrier, nx + ny - 2)

    small, ysmall, big = [], [], []
    for d in range(1, ny):
        to = lax.rem(gy + d, ny)
        small.append(remote(q_ref.at[to], q_in.at[d], qs.at[d], qr.at[d], (gx, to)))
    for d in range(1, nx):
        to = lax.rem(gx + d, nx)
        ysmall.append(remote(py_ref, y_in.at[d], ys.at[d], yr.at[d], (to, gy)))

    rows_b = per * span
    for b in range(batches):
        for d in range(1, ny + 1):
            to = lax.rem(gy + d, ny)
            for tile in range(lanes // 128):
                low = min(tile * 128 // per_c, a_in - 1)
                high = min((tile * 128 + 127) // per_c, a_in - 1)
                here = slice(tile * 128, tile * 128 + 128)
                weights = jnp.concatenate(
                    [gt_ref[to, :, here] * mask_ref[k : k + 1, here] for k in range(low, high + 1)], axis=0
                )
                left = w_ref[b * rows_b : (b + 1) * rows_b, low * deep : (high + 1) * deep]
                got = jnp.dot(left, weights, preferred_element_type=F32).astype(BF)
                u_buf[b, d - 1, :, :, here] = got.reshape(per, span, 128)
            target = r_ref.at[pl.ds(b * per, per), pl.ds(pl.multiple_of(gy * span, span), span), :]
            if d < ny:
                big.append(remote(u_buf.at[b, d - 1], target, us.at[b, d], ur.at[b, d], (gx, to)))
            else:
                own = pltpu.make_async_copy(u_buf.at[b, d - 1], target, ul.at[b])
                own.start()
                big.append(own)
        if b == 0:
            for copy in small:
                copy.wait()
            total = q_ref[gy]
            for d in range(1, ny):
                total = total + q_in[d]
            z_own[...] = total[x_rows:]
            zsmall = []
            for d in range(1, nx):
                to = lax.rem(gx + d, nx)
                zsmall.append(remote(z_own, z_in.at[d], zs.at[d], zr.at[d], (to, gy)))
            for copy in ysmall:
                copy.wait()
            y_in[0] = py_ref[...]
            y_total = jnp.zeros(py_ref.shape, F32)
            for g in range(nx):
                y_total = y_total + y_in[lax.rem(gx - g + nx, nx)]
            pyo_ref[...] = y_total
    for copy in zsmall:
        copy.wait()
    z_in[0] = z_own[...]
    z_total = jnp.zeros(z_own.shape, F32)
    for g in range(nx):
        z_total = z_total + z_in[lax.rem(gx - g + nx, nx)]
    q_all[gy, :x_rows] = total[:x_rows]
    q_all[gy, x_rows:] = z_total
    gathers = []
    for d in range(1, ny):
        to = lax.rem(gy + d, ny)
        gathers.append(remote(q_all.at[gy], q_all.at[gy], gs.at[d], gr.at[d], (gx, to)))
    for copy in gathers:
        copy.wait()
    qo_ref[...] = q_all[...]
    for copy in big:
        copy.wait()


def exchange(w, gt, mask, q, py, nx, ny, groups, span, per_c):
    batches = 3 if groups % 3 == 0 else 1
    per = groups // batches
    lanes = gt.shape[2]
    z_rows = gt.shape[1] // ny
    dma = lambda *shape: pltpu.SemaphoreType.DMA(shape)
    vm = pltpu.VMEM
    return pl.pallas_call(
        functools.partial(exchange_kernel, nx, ny, batches, per_c),
        out_shape=(
            jax.ShapeDtypeStruct((groups, ny * span, lanes), BF),
            jax.ShapeDtypeStruct(q.shape, F32),
            jax.ShapeDtypeStruct(py.shape, F32),
        ),
        in_specs=[VMEM] * 5,
        out_specs=(ANY, VMEM, VMEM),
        scratch_shapes=[
            vm((batches, ny, per, span, lanes), BF),
            vm(q.shape, F32), vm(q.shape, F32), vm((nx,) + py.shape, F32),
            vm((nx, z_rows, q.shape[2]), F32), vm((z_rows, q.shape[2]), F32),
            dma(batches, ny), dma(batches, ny), dma(batches),
            dma(ny), dma(ny), dma(nx), dma(nx), dma(nx), dma(nx), dma(ny), dma(ny),
        ],
        compiler_params=pltpu.CompilerParams(collective_id=1, has_side_effects=True),
    )(w, gt, mask, q, py)


def mix_y_kernel(r_ref, g_ref, o_ref):
    o_ref[0] = lax.dot_general(
        r_ref[0], g_ref[...], (((0,), (0,)), ((), ())), preferred_element_type=F32
    )


def mix_y(r, g):
    groups, deep, lanes = r.shape
    out = g.shape[1]
    return pl.pallas_call(
        mix_y_kernel,
        grid=(groups,),
        out_shape=jax.ShapeDtypeStruct((groups, lanes, out), F32),
        in_specs=[
            pl.BlockSpec((1, deep, lanes), lambda i: (i, 0, 0)),
            pl.BlockSpec((deep, out), lambda i: (0, 0)),
        ],
        out_specs=pl.BlockSpec((1, lanes, out), lambda i: (i, 0, 0)),
    )(r, g)


def per_device(
    nx, ny,
    thermal_field,
    probe_range_east,
    probe_range_north,
    probe_range_upward,
    gauss_kernel_east,
    gauss_kernel_north,
    gauss_kernel_upward,
):
    rows, span, deep = thermal_field.shape
    width = probe_range_upward.shape[1]
    a_rows = gauss_kernel_east.shape[0] // nx
    per_c = gauss_kernel_upward.shape[0] // ny
    a_in = 8 if a_rows % 8 == 0 and 8 * per_c % 128 == 0 else a_rows
    groups = a_rows // a_in
    used = a_in * per_c
    lanes = -(-used // 128) * 128

    w = mix_x(
        thermal_field.reshape(rows, span * deep),
        gauss_kernel_east.reshape(nx, a_rows, -1),
        nx,
        a_rows,
    )
    w = w.reshape(groups, a_in, span, deep).transpose(0, 2, 1, 3).reshape(groups * span, a_in * deep)

    unrolled = thermal_field.reshape(rows * span, deep)
    weighted = jnp.dot(unrolled, probe_range_upward, preferred_element_type=F32)
    weighted = weighted.reshape(rows, span, width)
    along_x = probe_range_east.astype(F32)
    along_y = probe_range_north.astype(F32)
    part_x = jnp.sum(weighted * along_y[None, :, :], axis=1)
    part_y = jnp.sum(weighted * along_x[:, None, :], axis=0)
    khatri = (along_x[:, None, :] * along_y[None, :, :]).astype(BF).reshape(rows * span, width)
    part_z = lax.dot_general(
        unrolled, khatri, (((0,), (0,)), ((), ())), preferred_element_type=F32
    )
    q = jnp.concatenate(
        [part_x.reshape(ny, rows // ny, width), part_z.reshape(ny, deep // ny, width)], axis=1
    )

    gt = gauss_kernel_upward.reshape(ny, per_c, deep).transpose(0, 2, 1)
    gt = jnp.pad(jnp.tile(gt, (1, 1, a_in)), ((0, 0), (0, 0), (0, lanes - used)))
    mask = (
        lax.broadcasted_iota(jnp.int32, (a_in, lanes), 1) // per_c
        == lax.broadcasted_iota(jnp.int32, (a_in, lanes), 0)
    ).astype(BF)
    r, q_sum, factor_y = exchange(w, gt, mask, q, part_y, nx, ny, groups, span, per_c)
    factor_x = q_sum[:, : rows // ny].reshape(rows, width)
    factor_z = q_sum[:, rows // ny :].reshape(deep, width)

    core = mix_y(r, gauss_kernel_north.T)
    core = core[:, :used].reshape(a_rows, per_c, -1).transpose(0, 2, 1)
    return (factor_x, factor_y, factor_z, core)


def solution(mesh):
    in_specs = (P("gx", "gy", None), P("gx", None), P("gy", None), P(), P(), P(), P())
    out_specs = (P("gx", None), P("gy", None), P(), P("gx", None, "gy"))
    body = functools.partial(per_device, mesh.shape["gx"], mesh.shape["gy"])
    return jax.shard_map(
        body, mesh=mesh, in_specs=in_specs, out_specs=out_specs, check_vma=False
    )
```

time: 265 us -> 149 us (0.56)
  blocking collectives: 159 us -> 0 us
  Pallas kernels: 0 us -> 132 us
  local copies, waits for them, and re-layouts: 49.3 us -> 9.74 us
  waiting for transfers between devices: 19.7 us -> 0 us
  between operations: 14.2 us -> 0.72 us
  matrix products: 13.7 us -> 2.98 us
  starting transfers between devices: 8.58 us -> 0 us
  other arithmetic: 0.01 us -> 2.74 us
    pallas_call x0 -> x3, Pallas kernels: none -> 132 us  [the longest x1 88.8 us: exchange(): pl.pallas_call(functools.partial(exchange_kernel, nx, ny, batches, per_c)...]
    psum x2 -> x0, blocking collectives: 119 us -> none  [the longest x1 106 us: per_device(): factor_x = lax.psum(part_x, 'gy')]
    all_to_all x2 -> x0, blocking collectives: 39.9 us -> none  [the longest x1 22.6 us: per_device(): lax.all_to_all(thermal_field, 'gx', split_axis=2, concat_axis=0, tiled=True)]
    all_to_all x6 -> x0, local copies, waits for them, and re-layouts: 22.7 us -> none  [the longest x2 13.1 us: per_device(): lax.all_to_all(mixed, 'gy', split_axis=2, concat_axis=1, tiled=True)]
    psum x1 -> x0, waiting for transfers between devices: 19.6 us -> none  [per_device(): factor_z = lax.psum(part_z, ('gx', 'gy'))]
    convert_element_type x2 -> x0, local copies, waits for them, and re-layouts: 12.3 us -> none  [the longest x1 7.02 us: per_device(): mixed = jnp.einsum('ajl,cl->ajc', lax.all_to_all(mixed, 'gx', split_axis=...]
    dot_general x5 -> x2, matrix products: 13.7 us -> 2.98 us  [the longest x1 1.84 us: per_device(): lax.dot_general(unrolled, khatri, (((0,), (0,)), ((), ())), preferred_ele...]
    unnamed x18 -> x14, local copies, waits for them, and re-layouts: 14.2 us -> 5.46 us
  transfers between devices with their start and end apart: 2 -> 0, of which waited for: 1 -> 0; matrix products, arithmetic and copies ran while one was open for 1% -> 0% of each run, Pallas kernels for 0% -> 0%
where the time goes in v2:
time: 149 us; the launch traced here: 148 us
  Pallas kernels  132 us (89%)
  local copies, waits for them, and re-layouts  9.74 us (7%)
  matrix products  2.98 us (2%)
  other arithmetic  2.74 us (2%)
    pallas_call x1, Pallas kernels, exchange(): pl.pallas_call(functools.partial(exchange_kernel, nx, ny, batches, per_c)...  88.8 us
    pallas_call x1, Pallas kernels, mix_x(): pl.pallas_call(functools.partial(mix_x_kernel, n, chunks), out_shape=jax....  32.5 us
    pallas_call x1, Pallas kernels, mix_y(): pl.pallas_call(mix_y_kernel, grid=(groups,), out_shape=jax.ShapeDtypeStru...  10.7 us
    unnamed x14, local copies, waits for them, and re-layouts  5.46 us

profile of v2, /device:TPU:1, one launch (start us, length us, event | category | flops | bytes accessed | tf_op | source)
XLA Modules:
  0.0 148.2 jit_solution(5852144670981700986)
XLA Ops:
  0.6 0.0 copy-start
  0.6 0.0 copy-start.1
  0.7 0.6 fusion.5.mask_ref
  1.3 0.7 convert_element_type.13
  2.0 0.7 convert_element_type.14
  2.7 1.8 %fusion = f32[128,128,1]{0,1,2:T(8,128)S(1)} fusion(bf16[96,48,128]{2,1,0:T(8,128)(2,1)} %param.7, f32[96,128]{1,0:T(8,128)S(1)} %convert_element_type.14, f32[48,128]{1,0:T(8,128)S(1)} %convert_element_type.13), kind=kOutput, calls=%fused_computation.3 | convolution fusion | flops 152174592 | bytes 1318912 | tf_op jit(solution)/shard_map/dot_general | solution.py:259
  4.6 0.0 copy-done
  4.6 0.0 copy-done.1
  4.6 0.0 copy-start.2
  4.6 0.0 copy-start.3
  4.6 1.1 multiply_reduce_fusion
  5.8 0.7 pad_maximum_fusion.q_ref
  6.4 0.0 copy-done.2
  6.4 0.9 copy.18
  7.3 0.0 copy-done.3
  7.3 0.1 tile.4
  7.4 1.2 copy.17.gt_ref
  8.6 1.3 copy.26
  9.9 32.5 %shard_map.102 = bf16[96,6144]{1,0:T(8,128)(2,1)} custom-call(bf16[96,6144]{1,0:T(8,128)(2,1)} %bitcast.37, bf16[4,96,384]{2,1,0:T(8,128)(2,1)} %bitcast.41), custom_call_target="tpu_custom_call" | custom-call | tf_op jit(solution)/shard_map/pallas_call | solution.py:76
  42.4 2.6 %copy.25 = bf16[72,8,8,128]{3,1,2,0:T(8,128)(2,1)} copy(bf16[72,8,8,128]{3,2,1,0:T(8,128)(2,1)} %bitcast.36) | data formatting | bytes 2359296
  45.0 88.8 %shard_map.103 = (bf16[12,384,384]{2,1,0:T(8,128)(2,1)}, f32[8,28,128]{2,1,0:T(8,128)}, f32[48,128]{1,0:T(8,128)}) custom-call(bf16[576,1024]{1,0:T(8,128)(2,1)} %bitcast.35, bf16[8,128,384]{2,1,0:T(8,128)(2,1)} %copy.17.gt_ref, bf16[8,384]{1,0:T(8,128)(2,1)} %fusion.5.mask_ref, f32[8,28,128]{2,1,0:T(8,128)} %pad_maximum_fusion.q_ref, ...), custom_call_target="tpu_custom_call" | custom-call | tf_op jit(solution)/shard_map/pallas_call | solution.py:183
  133.8 1.5 %slice.7 = f32[8,16,128]{2,1,0:T(8,128)} slice(f32[8,28,128]{2,1,0:T(8,128)} %get-tuple-element.7), slice={[0:8], [12:28], [0:128]} | slice | bytes 131072 | tf_op jit(solution)/shard_map/slice | solution.py:274
  135.4 0.8 slice.6
  136.2 0.6 reshape.56
  136.8 0.0 copy-start.4
  136.8 10.7 %shard_map.104 = f32[12,384,384]{2,1,0:T(8,128)} custom-call(bf16[12,384,384]{2,1,0:T(8,128)(2,1)} %get-tuple-element.9.r_ref, bf16[384,384]{1,0:T(8,128)(2,1)} %bitcast.39), custom_call_target="tpu_custom_call" | custom-call | tf_op jit(solution)/shard_map/pallas_call | solution.py:212
  147.6 0.0 copy-done.4
  147.6 0.6 copy.28
  (3 shorter events, 0.0 us)
Async XLA Ops:
  0.6 4.0 %copy-start = (bf16[128,128]{1,0:T(8,128)(2,1)S(1)}, bf16[128,128]{1,0:T(8,128)(2,1)}, u32[]{:S(2)}) copy-start(bf16[128,128]{1,0:T(8,128)(2,1)} %param.10) | copy-start | bytes 98308
  0.6 3.9 %copy-start.1 = (bf16[96,48,128]{2,1,0:T(8,128)(2,1)S(1)}, bf16[96,48,128]{2,1,0:T(8,128)(2,1)}, u32[]{:S(2)}) copy-start(bf16[96,48,128]{2,1,0:T(8,128)(2,1)} %param.7) | copy-start | bytes 3538948
  4.6 1.8 %copy-start.2 = (bf16[384,384]{1,0:T(8,128)(2,1)S(1)}, bf16[384,384]{1,0:T(8,128)(2,1)}, u32[]{:S(2)}) copy-start(bf16[384,384]{1,0:T(8,128)(2,1)} %param.12) | copy-start | bytes 884740
  4.6 2.7 %copy-start.3 = (bf16[384,128]{1,0:T(8,128)(2,1)S(1)}, bf16[384,128]{1,0:T(8,128)(2,1)}, u32[]{:S(2)}) copy-start(bf16[384,128]{1,0:T(8,128)(2,1)} %param.13) | copy-start | bytes 294916
  136.8 10.7 %copy-start.4 = (f32[48,128]{1,0:T(8,128)S(1)}, f32[48,128]{1,0:T(8,128)}, u32[]{:S(2)}) copy-start(f32[48,128]{1,0:T(8,128)} %get-tuple-element.19) | copy-start | bytes 73732

commit v3 on v2

--- a/solution.py
+++ b/solution.py
@@ -173,15 +173,222 @@
         copy.wait()
 
 
+def line_kernel(
+    nx, ny, batches, per_c, w_ref, gt_ref, mask_ref, q_ref, py_ref,
+    r_ref, qo_ref, pyo_ref,
+    w_in, u_buf, wt, q_in, q_all, y_in, z_in, z_own,
+    ws, wr, us, ur, ul, qs, qr, ys, yr, zs, zr, gs, gr,
+):
+    gx, gy = lax.axis_index("gx"), lax.axis_index("gy")
+    spot, core = gy // 2, gy % 2
+    last = ny // 2 - 1
+    middle = jnp.logical_and(spot > 0, spot < last)
+    left_half = spot * 2 < last
+    end = jnp.where(left_half, 0, last)
+    near = jnp.where(left_half, 1, last - 1)
+    _, _, _, per, span, lanes = u_buf.shape
+    a_in = mask_ref.shape[0]
+    deep = gt_ref.shape[1]
+    x_rows = q_ref.shape[1] - z_in.shape[1]
+    rows_b = per * span
+    spots = (end, last - spot, last - end, spot)
+    goals = (gy, 2 * spot + 1 - core, 2 * end, 2 * end + 1)
+    barrier = pltpu.get_barrier_semaphore()
+    for d in range(1, ny):
+        pl.semaphore_signal(barrier, inc=1, device_id=(gx, lax.rem(gy + d, ny)), device_id_type=MESH)
+    for d in range(1, nx):
+        pl.semaphore_signal(barrier, inc=1, device_id=(lax.rem(gx + d, nx), gy), device_id_type=MESH)
+    pl.semaphore_wait(barrier, nx + ny - 2)
+
+    small, ysmall = [], []
+    for d in range(1, ny):
+        to = lax.rem(gy + d, ny)
+        small.append(remote(q_ref.at[to], q_in.at[d], qs.at[d], qr.at[d], (gx, to)))
+    for d in range(1, nx):
+        to = lax.rem(gx + d, nx)
+        ysmall.append(remote(py_ref, y_in.at[d], ys.at[d], yr.at[d], (to, gy)))
+
+    def raw(src, slot, b, to_spot):
+        return pltpu.make_async_remote_copy(
+            src_ref=src, dst_ref=w_in.at[slot, b], send_sem=ws.at[slot, b], recv_sem=wr.at[slot, b],
+            device_id=(gx, 2 * to_spot + core), device_id_type=MESH,
+        )
+
+    def rows_of(b):
+        return w_ref.at[pl.ds(b * rows_b, rows_b), :]
+
+    def place(b, origin):
+        return r_ref.at[pl.ds(b * per, per), pl.ds(pl.multiple_of(origin * span, span), span), :]
+
+    def block(kind, slot, b):
+        source = 2 * spots[slot] + core
+        if kind == 0:
+            return pltpu.make_async_copy(u_buf.at[kind, slot, b], place(b, source), ul.at[slot, b])
+        return pltpu.make_async_remote_copy(
+            src_ref=u_buf.at[kind, slot, b], dst_ref=place(b, source),
+            send_sem=us.at[kind, slot, b], recv_sem=ur.at[b, spots[slot], core],
+            device_id=(gx, goals[kind]), device_id_type=MESH,
+        )
+
+    def arrived(b, at, side):
+        pltpu.make_async_remote_copy(
+            src_ref=u_buf.at[0, 0, b], dst_ref=place(b, 2 * at + side),
+            send_sem=us.at[1, 0, b], recv_sem=ur.at[b, at, side],
+            device_id=(gx, goals[1]), device_id_type=MESH,
+        ).wait_recv()
+
+    pieces, base = [], 0
+    for tile in range(lanes // 128):
+        low = min(tile * 128 // per_c, a_in - 1)
+        high = min((tile * 128 + 127) // per_c, a_in - 1)
+        pieces.append((tile, low, high, base))
+        base += (high + 1 - low) * deep
+
+    def weigh(kind):
+        for tile, low, high, at in pieces:
+            here = slice(tile * 128, tile * 128 + 128)
+            for k in range(low, high + 1):
+                wt[kind, at + (k - low) * deep : at + (k - low + 1) * deep] = (
+                    gt_ref[goals[kind], :, here] * mask_ref[k : k + 1, here]
+                )
+
+    def mix(kind, slot, b, left):
+        for tile, low, high, at in pieces:
+            got = jnp.dot(
+                left[:, low * deep : (high + 1) * deep],
+                wt[kind, at : at + (high + 1 - low) * deep],
+                preferred_element_type=F32,
+            ).astype(BF)
+            u_buf[kind, slot, b, :, :, tile * 128 : tile * 128 + 128] = got.reshape(per, span, 128)
+
+    def own_blocks(kind):
+        weigh(kind)
+        for b in range(batches):
+            mix(kind, 3, b, rows_of(b))
+            block(kind, 3, b).start()
+
+    @pl.when(middle)
+    def _():
+        for b in range(batches):
+            raw(rows_of(b), 1, b, last - spot).start()
+        for kind in (2, 3):
+            own_blocks(kind)
+
+    @pl.when(jnp.logical_not(middle))
+    def _():
+        for b in range(batches):
+            raw(rows_of(b), 0, b, near).start()
+
+    for kind in (1, 0):
+        own_blocks(kind)
+
+    for copy in small:
+        copy.wait()
+    total = q_ref[gy]
+    for d in range(1, ny):
+        total = total + q_in[d]
+    z_own[...] = total[x_rows:]
+    zsmall = []
+    for d in range(1, nx):
+        to = lax.rem(gx + d, nx)
+        zsmall.append(remote(z_own, z_in.at[d], zs.at[d], zr.at[d], (to, gy)))
+    for copy in ysmall:
+        copy.wait()
+    y_in[0] = py_ref[...]
+    y_total = jnp.zeros(py_ref.shape, F32)
+    for g in range(nx):
+        y_total = y_total + y_in[lax.rem(gx - g + nx, nx)]
+    pyo_ref[...] = y_total
+    for copy in zsmall:
+        copy.wait()
+    z_in[0] = z_own[...]
+    z_total = jnp.zeros(z_own.shape, F32)
+    for g in range(nx):
+        z_total = z_total + z_in[lax.rem(gx - g + nx, nx)]
+    q_all[gy, :x_rows] = total[:x_rows]
+    q_all[gy, x_rows:] = z_total
+    gathers = []
+    for d in range(1, ny):
+        to = lax.rem(gy + d, ny)
+        gathers.append(remote(q_all.at[gy], q_all.at[gy], gs.at[d], gr.at[d], (gx, to)))
+
+    @pl.when(middle)
+    def _():
+        for b in range(batches):
+            raw(rows_of(b), 0, b, near).wait_recv()
+            raw(w_in.at[0, b], 2, b, last - spot).start()
+            raw(rows_of(b), 1, b, last - spot).wait_recv()
+            for kind, slot in ((2, 1), (3, 1), (1, 1), (1, 0), (0, 1), (0, 0)):
+                mix(kind, slot, b, w_in.at[slot, b])
+                block(kind, slot, b).start()
+        for b in range(batches):
+            raw(w_in.at[0, b], 2, b, last - spot).wait_recv()
+            for kind in (2, 3, 1, 0):
+                mix(kind, 2, b, w_in.at[2, b])
+                block(kind, 2, b).start()
+        for b in range(batches):
+            raw(rows_of(b), 1, b, last - spot).wait_send()
+            raw(w_in.at[0, b], 2, b, last - spot).wait_send()
+            for slot in range(4):
+                block(0, slot, b).wait()
+                block(1, slot, b).wait_send()
+                if slot:
+                    block(2, slot, b).wait_send()
+                    block(3, slot, b).wait_send()
+                arrived(b, spots[slot], 1 - core)
+
+    @pl.when(jnp.logical_not(middle))
+    def _():
+        for b in range(batches):
+            raw(rows_of(b), 0, b, near).wait_send()
+            block(0, 3, b).wait()
+            block(1, 3, b).wait_send()
+            arrived(b, spot, 1 - core)
+            for d in range(1, ny // 2):
+                for side in range(2):
+                    arrived(b, lax.rem(spot + d, ny // 2), side)
+
+    for copy in gathers:
+        copy.wait()
+    qo_ref[...] = q_all[...]
+
+
 def exchange(w, gt, mask, q, py, nx, ny, groups, span, per_c):
-    batches = 3 if groups % 3 == 0 else 1
-    per = groups // batches
     lanes = gt.shape[2]
-    z_rows = gt.shape[1] // ny
+    deep = gt.shape[1]
+    z_rows = deep // ny
     dma = lambda *shape: pltpu.SemaphoreType.DMA(shape)
     vm = pltpu.VMEM
+    sums = [
+        vm(q.shape, F32), vm(q.shape, F32), vm((nx,) + py.shape, F32),
+        vm((nx, z_rows, q.shape[2]), F32), vm((z_rows, q.shape[2]), F32),
+    ]
+    sum_sems = [dma(ny), dma(ny), dma(nx), dma(nx), dma(nx), dma(nx), dma(ny), dma(ny)]
+    if ny == 8 and groups % 4 == 0:
+        batches = 4
+        per = groups // batches
+        total_k = sum(
+            min((t * 128 + 127) // per_c, mask.shape[0] - 1) + 1 - t * 128 // per_c
+            for t in range(lanes // 128)
+        ) * deep
+        body = functools.partial(line_kernel, nx, ny, batches, per_c)
+        scratch = [
+            vm((3, batches, per * span, w.shape[1]), BF),
+            vm((4, 4, batches, per, span, lanes), BF),
+            vm((4, total_k, 128), BF),
+        ] + sums + [
+            dma(3, batches), dma(3, batches), dma(4, 4, batches), dma(batches, ny // 2, 2),
+            dma(4, batches),
+        ] + sum_sems
+    else:
+        batches = 3 if groups % 3 == 0 else 1
+        per = groups // batches
+        body = functools.partial(exchange_kernel, nx, ny, batches, per_c)
+        scratch = [vm((batches, ny, per, span, lanes), BF)] + sums + [
+            dma(batches, ny), dma(batches, ny), dma(batches)
+        ] + sum_sems
     return pl.pallas_call(
-        functools.partial(exchange_kernel, nx, ny, batches, per_c),
+        body,
         out_shape=(
             jax.ShapeDtypeStruct((groups, ny * span, lanes), BF),
             jax.ShapeDtypeStruct(q.shape, F32),
@@ -189,13 +396,7 @@
         ),
         in_specs=[VMEM] * 5,
         out_specs=(ANY, VMEM, VMEM),
-        scratch_shapes=[
-            vm((batches, ny, per, span, lanes), BF),
-            vm(q.shape, F32), vm(q.shape, F32), vm((nx,) + py.shape, F32),
-            vm((nx, z_rows, q.shape[2]), F32), vm((z_rows, q.shape[2]), F32),
-            dma(batches, ny), dma(batches, ny), dma(batches),
-            dma(ny), dma(ny), dma(nx), dma(nx), dma(nx), dma(nx), dma(ny), dma(ny),
-        ],
+        scratch_shapes=scratch,
         compiler_params=pltpu.CompilerParams(collective_id=1, has_side_effects=True),
     )(w, gt, mask, q, py)
 

time: 149 us -> 130 us (0.87)
  Pallas kernels: 132 us -> 113 us
    pallas_call x1, Pallas kernels: 88.8 us -> 70.2 us  [exchange(): pl.pallas_call(body, out_shape=(jax.ShapeDtypeStruct((groups, ny * span,...]
where the time goes in v3:
time: 130 us
  Pallas kernels  113 us (87%)
  local copies, waits for them, and re-layouts  9.74 us (7%)
  matrix products  2.99 us (2%)
  other arithmetic  2.74 us (2%)
    pallas_call x1, Pallas kernels, exchange(): pl.pallas_call(body, out_shape=(jax.ShapeDtypeStruct((groups, ny * span,...  70.2 us
    pallas_call x1, Pallas kernels, mix_x(): pl.pallas_call(functools.partial(mix_x_kernel, n, chunks), out_shape=jax....  32.5 us
    pallas_call x1, Pallas kernels, mix_y(): pl.pallas_call(mix_y_kernel, grid=(groups,), out_shape=jax.ShapeDtypeStru...  10.7 us
    unnamed x14, local copies, waits for them, and re-layouts  5.46 us

profile of v3, /device:TPU:1, one launch (start us, length us, event | category | flops | bytes accessed | tf_op | source)
XLA Modules:
  0.0 129.6 jit_solution(8075451690840558924)
XLA Ops:
  0.6 0.0 copy-start
  0.6 0.0 copy-start.1
  0.7 0.6 fusion.5.mask_ref
  1.3 0.7 convert_element_type.13
  2.0 0.7 convert_element_type.14
  2.7 1.8 %fusion = f32[128,128,1]{0,1,2:T(8,128)S(1)} fusion(bf16[96,48,128]{2,1,0:T(8,128)(2,1)} %param.7, f32[96,128]{1,0:T(8,128)S(1)} %convert_element_type.14, f32[48,128]{1,0:T(8,128)S(1)} %convert_element_type.13), kind=kOutput, calls=%fused_computation.3 | convolution fusion | flops 152174592 | bytes 1318912 | tf_op jit(solution)/shard_map/dot_general | solution.py:460
  4.6 0.0 copy-done
  4.6 0.0 copy-done.1
  4.6 0.0 copy-start.2
  4.6 0.0 copy-start.3
  4.6 1.2 multiply_reduce_fusion
  5.8 0.7 pad_maximum_fusion.q_ref
  6.5 0.0 copy-done.2
  6.5 0.9 copy.18
  7.3 0.0 copy-done.3
  7.3 0.1 tile.4
  7.5 1.2 copy.17.gt_ref
  8.6 1.3 %copy.26 = bf16[12,8,48,128]{3,1,2,0:T(8,128)(2,1)} copy(bf16[12,8,48,128]{3,2,1,0:T(8,128)(2,1)S(1)} %bitcast.40) | data formatting | bytes 2359296
  9.9 32.5 %shard_map.102 = bf16[96,6144]{1,0:T(8,128)(2,1)} custom-call(bf16[96,6144]{1,0:T(8,128)(2,1)} %bitcast.37, bf16[4,96,384]{2,1,0:T(8,128)(2,1)} %bitcast.41), custom_call_target="tpu_custom_call" | custom-call | tf_op jit(solution)/shard_map/pallas_call | solution.py:76
  42.4 2.6 %copy.25 = bf16[72,8,8,128]{3,1,2,0:T(8,128)(2,1)} copy(bf16[72,8,8,128]{3,2,1,0:T(8,128)(2,1)} %bitcast.36) | data formatting | bytes 2359296
  45.0 70.2 %shard_map.103 = (bf16[12,384,384]{2,1,0:T(8,128)(2,1)}, f32[8,28,128]{2,1,0:T(8,128)}, f32[48,128]{1,0:T(8,128)}) custom-call(bf16[576,1024]{1,0:T(8,128)(2,1)} %bitcast.35, bf16[8,128,384]{2,1,0:T(8,128)(2,1)} %copy.17.gt_ref, bf16[8,384]{1,0:T(8,128)(2,1)} %fusion.5.mask_ref, f32[8,28,128]{2,1,0:T(8,128)} %pad_maximum_fusion.q_ref, ...), custom_call_target="tpu_custom_call" | custom-call | tf_op jit(solution)/shard_map/pallas_call | solution.py:390
  115.3 1.5 %slice.7 = f32[8,16,128]{2,1,0:T(8,128)} slice(f32[8,28,128]{2,1,0:T(8,128)} %get-tuple-element.7), slice={[0:8], [12:28], [0:128]} | slice | bytes 131072 | tf_op jit(solution)/shard_map/slice | solution.py:475
  116.8 0.8 slice.6
  117.7 0.6 reshape.56
  118.3 0.0 copy-start.4
  118.3 10.7 %shard_map.104 = f32[12,384,384]{2,1,0:T(8,128)} custom-call(bf16[12,384,384]{2,1,0:T(8,128)(2,1)} %get-tuple-element.9.r_ref, bf16[384,384]{1,0:T(8,128)(2,1)} %bitcast.39), custom_call_target="tpu_custom_call" | custom-call | tf_op jit(solution)/shard_map/pallas_call | solution.py:413
  129.0 0.0 copy-done.4
  129.0 0.6 copy.28
  (3 shorter events, 0.0 us)
Async XLA Ops:
  0.6 4.0 %copy-start = (bf16[128,128]{1,0:T(8,128)(2,1)S(1)}, bf16[128,128]{1,0:T(8,128)(2,1)}, u32[]{:S(2)}) copy-start(bf16[128,128]{1,0:T(8,128)(2,1)} %param.10) | copy-start | bytes 98308
  0.6 3.9 %copy-start.1 = (bf16[96,48,128]{2,1,0:T(8,128)(2,1)S(1)}, bf16[96,48,128]{2,1,0:T(8,128)(2,1)}, u32[]{:S(2)}) copy-start(bf16[96,48,128]{2,1,0:T(8,128)(2,1)} %param.7) | copy-start | bytes 3538948
  4.6 1.9 %copy-start.2 = (bf16[384,384]{1,0:T(8,128)(2,1)S(1)}, bf16[384,384]{1,0:T(8,128)(2,1)}, u32[]{:S(2)}) copy-start(bf16[384,384]{1,0:T(8,128)(2,1)} %param.12) | copy-start | bytes 884740
  4.6 2.7 %copy-start.3 = (bf16[384,128]{1,0:T(8,128)(2,1)S(1)}, bf16[384,128]{1,0:T(8,128)(2,1)}, u32[]{:S(2)}) copy-start(bf16[384,128]{1,0:T(8,128)(2,1)} %param.13) | copy-start | bytes 294916
  118.3 10.7 %copy-start.4 = (f32[48,128]{1,0:T(8,128)S(1)}, f32[48,128]{1,0:T(8,128)}, u32[]{:S(2)}) copy-start(f32[48,128]{1,0:T(8,128)} %get-tuple-element.19) | copy-start | bytes 73732

commit v4 on v3

--- a/solution.py
+++ b/solution.py
@@ -22,7 +22,35 @@
     return copy
 
 
-def mix_x_kernel(n, chunks, t_ref, g_ref, w_ref, x_buf, y_buf, s1, r1, s2, r2, ls):
+def sketch_parts(f_ref, east_ref, north_ref, up_ref, q_ref, py_ref, px_buf):
+    rows, span, deep = f_ref.shape
+    width = up_ref.shape[1]
+    step = 16 if rows % 16 == 0 else rows
+    along_y = north_ref[...].astype(F32)
+    part_y = jnp.zeros((span, width), F32)
+    part_z = jnp.zeros((deep, width), F32)
+    for c in range(0, rows, step):
+        cells = f_ref[c : c + step].reshape(step * span, deep)
+        along_x = east_ref[c : c + step].astype(F32)
+        weighted = jnp.dot(cells, up_ref[...], preferred_element_type=F32).reshape(step, span, width)
+        px_buf[c : c + step] = jnp.sum(weighted * along_y[None, :, :], axis=1)
+        part_y = part_y + jnp.sum(weighted * along_x[:, None, :], axis=0)
+        khatri = (along_x[:, None, :] * along_y[None, :, :]).astype(BF).reshape(step * span, width)
+        part_z = part_z + lax.dot_general(
+            cells, khatri, (((0,), (0,)), ((), ())), preferred_element_type=F32
+        )
+    py_ref[...] = part_y
+    ny = q_ref.shape[0]
+    x_rows, z_rows = rows // ny, deep // ny
+    for k in range(ny):
+        q_ref[k, :x_rows] = px_buf[k * x_rows : (k + 1) * x_rows]
+        q_ref[k, x_rows:] = part_z[k * z_rows : (k + 1) * z_rows]
+
+
+def mix_x_kernel(
+    n, chunks, t_ref, g_ref, f_ref, east_ref, north_ref, up_ref, w_ref, q_ref, py_ref,
+    x_buf, y_buf, px_buf, s1, r1, s2, r2, ls,
+):
     gx, gy = lax.axis_index("gx"), lax.axis_index("gy")
     rows = t_ref.shape[0]
     a_rows = y_buf.shape[2]
@@ -45,6 +73,7 @@
         own = pltpu.make_async_copy(t_ref.at[:, lanes], x_buf.at[m, gx], ls.at[m, 0])
         own.start()
         local.append(own)
+    sketch_parts(f_ref, east_ref, north_ref, up_ref, q_ref, py_ref, px_buf)
     for m in range(chunks):
         local[m].wait()
         for d in range(1, n):
@@ -68,28 +97,33 @@
         copy.wait()
 
 
-def mix_x(field, gauss, n, a_rows):
+def mix_x(field, gauss, n, a_rows, cells, east, north, up, ny):
     rows, lanes = field.shape
     wide = lanes // n
     chunks = 3 if wide % 384 == 0 else 1
     dma = lambda *shape: pltpu.SemaphoreType.DMA(shape)
     return pl.pallas_call(
         functools.partial(mix_x_kernel, n, chunks),
-        out_shape=jax.ShapeDtypeStruct((a_rows, lanes), BF),
-        in_specs=[VMEM, VMEM],
-        out_specs=VMEM,
+        out_shape=(
+            jax.ShapeDtypeStruct((a_rows, lanes), BF),
+            jax.ShapeDtypeStruct((ny, (cells.shape[0] + cells.shape[2]) // ny, up.shape[1]), F32),
+            jax.ShapeDtypeStruct(north.shape, F32),
+        ),
+        in_specs=[VMEM] * 6,
+        out_specs=(VMEM, VMEM, VMEM),
         scratch_shapes=[
             pltpu.VMEM((chunks, n, rows, wide // chunks), BF),
             pltpu.VMEM((chunks, n, a_rows, wide // chunks), BF),
+            pltpu.VMEM(east.shape, F32),
             dma(chunks, n), dma(chunks, n), dma(chunks, n), dma(chunks, n), dma(chunks, 2),
         ],
         compiler_params=pltpu.CompilerParams(collective_id=0, has_side_effects=True),
-    )(field, gauss)
+    )(field, gauss, cells, east, north, up)
 
 
 def exchange_kernel(
     nx, ny, batches, per_c, w_ref, gt_ref, mask_ref, q_ref, py_ref,
-    r_ref, qo_ref, pyo_ref,
+    r_ref, fx_ref, fz_ref, pyo_ref,
     u_buf, q_in, q_all, y_in, z_in, z_own,
     us, ur, ul, qs, qr, ys, yr, zs, zr, gs, gr,
 ):
@@ -168,14 +202,17 @@
         gathers.append(remote(q_all.at[gy], q_all.at[gy], gs.at[d], gr.at[d], (gx, to)))
     for copy in gathers:
         copy.wait()
-    qo_ref[...] = q_all[...]
+    z_rows = z_own.shape[0]
+    for k in range(ny):
+        fx_ref[k * x_rows : (k + 1) * x_rows] = q_all[k, :x_rows]
+        fz_ref[k * z_rows : (k + 1) * z_rows] = q_all[k, x_rows:]
     for copy in big:
         copy.wait()
 
 
 def line_kernel(
     nx, ny, batches, per_c, w_ref, gt_ref, mask_ref, q_ref, py_ref,
-    r_ref, qo_ref, pyo_ref,
+    r_ref, fx_ref, fz_ref, pyo_ref,
     w_in, u_buf, wt, q_in, q_all, y_in, z_in, z_own,
     ws, wr, us, ur, ul, qs, qr, ys, yr, zs, zr, gs, gr,
 ):
@@ -350,7 +387,10 @@
 
     for copy in gathers:
         copy.wait()
-    qo_ref[...] = q_all[...]
+    z_rows = z_own.shape[0]
+    for k in range(ny):
+        fx_ref[k * x_rows : (k + 1) * x_rows] = q_all[k, :x_rows]
+        fz_ref[k * z_rows : (k + 1) * z_rows] = q_all[k, x_rows:]
 
 
 def exchange(w, gt, mask, q, py, nx, ny, groups, span, per_c):
@@ -391,34 +431,37 @@
         body,
         out_shape=(
             jax.ShapeDtypeStruct((groups, ny * span, lanes), BF),
-            jax.ShapeDtypeStruct(q.shape, F32),
+            jax.ShapeDtypeStruct((ny * q.shape[1] - deep, q.shape[2]), F32),
+            jax.ShapeDtypeStruct((deep, q.shape[2]), F32),
             jax.ShapeDtypeStruct(py.shape, F32),
         ),
         in_specs=[VMEM] * 5,
-        out_specs=(ANY, VMEM, VMEM),
+        out_specs=(ANY, VMEM, VMEM, VMEM),
         scratch_shapes=scratch,
         compiler_params=pltpu.CompilerParams(collective_id=1, has_side_effects=True),
     )(w, gt, mask, q, py)
 
 
 def mix_y_kernel(r_ref, g_ref, o_ref):
-    o_ref[0] = lax.dot_general(
-        r_ref[0], g_ref[...], (((0,), (0,)), ((), ())), preferred_element_type=F32
-    )
+    for k in range(r_ref.shape[0]):
+        o_ref[k] = lax.dot_general(
+            r_ref[k], g_ref[...], (((0,), (0,)), ((), ())), preferred_element_type=F32
+        )
 
 
 def mix_y(r, g):
     groups, deep, lanes = r.shape
     out = g.shape[1]
+    take = 2 if groups % 2 == 0 else 1
     return pl.pallas_call(
         mix_y_kernel,
-        grid=(groups,),
+        grid=(groups // take,),
         out_shape=jax.ShapeDtypeStruct((groups, lanes, out), F32),
         in_specs=[
-            pl.BlockSpec((1, deep, lanes), lambda i: (i, 0, 0)),
+            pl.BlockSpec((take, deep, lanes), lambda i: (i, 0, 0)),
             pl.BlockSpec((deep, out), lambda i: (0, 0)),
         ],
-        out_specs=pl.BlockSpec((1, lanes, out), lambda i: (i, 0, 0)),
+        out_specs=pl.BlockSpec((take, lanes, out), lambda i: (i, 0, 0)),
     )(r, g)
 
 
@@ -433,7 +476,6 @@
     gauss_kernel_upward,
 ):
     rows, span, deep = thermal_field.shape
-    width = probe_range_upward.shape[1]
     a_rows = gauss_kernel_east.shape[0] // nx
     per_c = gauss_kernel_upward.shape[0] // ny
     a_in = 8 if a_rows % 8 == 0 and 8 * per_c % 128 == 0 else a_rows
@@ -441,28 +483,18 @@
     used = a_in * per_c
     lanes = -(-used // 128) * 128
 
-    w = mix_x(
+    w, q, part_y = mix_x(
         thermal_field.reshape(rows, span * deep),
         gauss_kernel_east.reshape(nx, a_rows, -1),
         nx,
         a_rows,
+        thermal_field,
+        probe_range_east,
+        probe_range_north,
+        probe_range_upward,
+        ny,
     )
     w = w.reshape(groups, a_in, span, deep).transpose(0, 2, 1, 3).reshape(groups * span, a_in * deep)
-
-    unrolled = thermal_field.reshape(rows * span, deep)
-    weighted = jnp.dot(unrolled, probe_range_upward, preferred_element_type=F32)
-    weighted = weighted.reshape(rows, span, width)
-    along_x = probe_range_east.astype(F32)
-    along_y = probe_range_north.astype(F32)
-    part_x = jnp.sum(weighted * along_y[None, :, :], axis=1)
-    part_y = jnp.sum(weighted * along_x[:, None, :], axis=0)
-    khatri = (along_x[:, None, :] * along_y[None, :, :]).astype(BF).reshape(rows * span, width)
-    part_z = lax.dot_general(
-        unrolled, khatri, (((0,), (0,)), ((), ())), preferred_element_type=F32
-    )
-    q = jnp.concatenate(
-        [part_x.reshape(ny, rows // ny, width), part_z.reshape(ny, deep // ny, width)], axis=1
-    )
 
     gt = gauss_kernel_upward.reshape(ny, per_c, deep).transpose(0, 2, 1)
     gt = jnp.pad(jnp.tile(gt, (1, 1, a_in)), ((0, 0), (0, 0), (0, lanes - used)))
@@ -470,9 +502,7 @@
         lax.broadcasted_iota(jnp.int32, (a_in, lanes), 1) // per_c
         == lax.broadcasted_iota(jnp.int32, (a_in, lanes), 0)
     ).astype(BF)
-    r, q_sum, factor_y = exchange(w, gt, mask, q, part_y, nx, ny, groups, span, per_c)
-    factor_x = q_sum[:, : rows // ny].reshape(rows, width)
-    factor_z = q_sum[:, rows // ny :].reshape(deep, width)
+    r, factor_x, factor_z, factor_y = exchange(w, gt, mask, q, part_y, nx, ny, groups, span, per_c)
 
     core = mix_y(r, gauss_kernel_north.T)
     core = core[:, :used].reshape(a_rows, per_c, -1).transpose(0, 2, 1)

time: 130 us -> 122 us (0.938)
  matrix products: 2.99 us -> 0 us
  other arithmetic: 2.74 us -> 0.62 us
  Pallas kernels: 113 us -> 111 us
    dot_general x2 -> x0, matrix products: 2.99 us -> none  [the longest x1 1.84 us: per_device(): lax.dot_general(unrolled, khatri, (((0,), (0,)), ((), ())), preferred_ele...]
    pallas_call x2, Pallas kernels: 43.2 us -> 40.5 us  [the longest x1 33 us: mix_x(): pl.pallas_call(functools.partial(mix_x_kernel, n, chunks), out_shape=(jax...]
    slice x2 -> x0, local copies, waits for them, and re-layouts: 2.38 us -> none  [the longest x1 1.53 us: per_device(): factor_z = q_sum[:, rows // ny:].reshape(deep, width)]
    unnamed x14, local copies, waits for them, and re-layouts: 5.46 us -> 7.65 us
    convert_element_type x2 -> x0, other arithmetic: 1.45 us -> none  [the longest x1 0.74 us: per_device(): along_x = probe_range_east.astype(F32)]
where the time goes in v4:
time: 122 us
  Pallas kernels  111 us (91%)
  local copies, waits for them, and re-layouts  9.9 us (8%)
    pallas_call x1, Pallas kernels, exchange(): pl.pallas_call(body, out_shape=(jax.ShapeDtypeStruct((groups, ny * span,...  70.2 us
    pallas_call x1, Pallas kernels, mix_x(): pl.pallas_call(functools.partial(mix_x_kernel, n, chunks), out_shape=(jax...  33 us
    unnamed x14, local copies, waits for them, and re-layouts  7.65 us
    pallas_call x1, Pallas kernels, mix_y(): pl.pallas_call(mix_y_kernel, grid=(groups // take,), out_shape=jax.ShapeD...  7.49 us

profile of v4, /device:TPU:1, one launch (start us, length us, event | category | flops | bytes accessed | tf_op | source)
XLA Modules:
  0.0 121.9 jit_solution(908642598051573842)
XLA Ops:
  0.7 0.6 fusion.mask_ref
  1.3 1.8 %copy.14 = bf16[384,384]{0,1:T(8,128)(2,1)} copy(bf16[384,384]{1,0:T(8,128)(2,1)} %param.12) | data formatting | bytes 589824 | tf_op args[5]
  3.1 0.0 copy-start
  3.1 1.1 tile.4
  4.2 1.2 copy.13.gt_ref
  5.4 0.0 copy-done
  5.4 1.3 %copy.20 = bf16[12,8,48,128]{3,1,2,0:T(8,128)(2,1)} copy(bf16[12,8,48,128]{3,2,1,0:T(8,128)(2,1)S(1)} %bitcast.23) | data formatting | bytes 2359296
  6.7 33.0 %shard_map.102 = (bf16[96,6144]{1,0:T(8,128)(2,1)}, f32[8,28,128]{2,1,0:T(8,128)}, f32[48,128]{1,0:T(8,128)}) custom-call(bf16[96,6144]{1,0:T(8,128)(2,1)} %bitcast.24, bf16[4,96,384]{2,1,0:T(8,128)(2,1)} %bitcast.28, bf16[96,48,128]{2,1,0:T(8,128)(2,1)} %f_ref.1, bf16[96,128]{1,0:T(8,128)(2,1)} %east_ref.1, bf16[48,128]{1,0:T(8,128)(2,1)} %north_ref.1, ...), custom_call_target="tpu_custom_call" | custom-call | tf_op jit(solution)/shard_map/pallas_call | solution.py:105
  39.7 2.6 %copy.19 = bf16[72,8,8,128]{3,1,2,0:T(8,128)(2,1)} copy(bf16[72,8,8,128]{3,2,1,0:T(8,128)(2,1)} %bitcast.27) | data formatting | bytes 2359296
  42.3 70.2 %shard_map.103 = (bf16[12,384,384]{2,1,0:T(8,128)(2,1)}, f32[96,128]{1,0:T(8,128)}, f32[128,128]{1,0:T(8,128)}, f32[48,128]{1,0:T(8,128)}) custom-call(bf16[576,1024]{1,0:T(8,128)(2,1)} %bitcast.22, bf16[8,128,384]{2,1,0:T(8,128)(2,1)} %copy.13.gt_ref, bf16[8,384]{1,0:T(8,128)(2,1)} %fusion.mask_ref, f32[8,28,128]{2,1,0:T(8,128)} %get-tuple-element.12.q_ref, ...), custom_call_target="tpu_custom_call" | custom-call | tf_op jit(solution)/shard_map/pallas_call | solution.py:430
  112.5 0.0 copy-start.2
  112.5 0.0 copy-start.3
  112.5 0.0 copy-start.1
  112.5 7.5 %shard_map.104 = f32[12,384,384]{2,1,0:T(8,128)} custom-call(bf16[12,384,384]{2,1,0:T(8,128)(2,1)} %get-tuple-element.17.r_ref, bf16[384,384]{1,0:T(8,128)(2,1)} %bitcast.26), custom_call_target="tpu_custom_call" | custom-call | tf_op jit(solution)/shard_map/pallas_call | solution.py:456
  120.0 0.0 copy-done.2
  120.0 0.6 copy.24
  120.7 0.0 copy-done.3
  120.7 0.6 copy.25
  121.3 0.0 copy-done.1
  121.3 0.6 copy.26
  (2 shorter events, 0.0 us)
Async XLA Ops:
  3.1 2.3 %copy-start = (bf16[96,48,128]{2,1,0:T(8,128)(2,1)S(1)}, bf16[96,48,128]{2,1,0:T(8,128)(2,1)}, u32[]{:S(2)}) copy-start(bf16[96,48,128]{2,1,0:T(8,128)(2,1)} %f_ref.1) | copy-start | bytes 3538948
  112.5 7.5 %copy-start.2 = (f32[96,128]{1,0:T(8,128)S(1)}, f32[96,128]{1,0:T(8,128)}, u32[]{:S(2)}) copy-start(f32[96,128]{1,0:T(8,128)} %get-tuple-element.24) | copy-start | bytes 147460
  112.5 8.1 %copy-start.3 = (f32[48,128]{1,0:T(8,128)S(1)}, f32[48,128]{1,0:T(8,128)}, u32[]{:S(2)}) copy-start(f32[48,128]{1,0:T(8,128)} %get-tuple-element.25) | copy-start | bytes 73732
  112.5 8.7 %copy-start.1 = (f32[128,128]{1,0:T(8,128)S(1)}, f32[128,128]{1,0:T(8,128)}, u32[]{:S(2)}) copy-start(f32[128,128]{1,0:T(8,128)} %get-tuple-element.26) | copy-start | bytes 196612

commit v5 on v4

--- a/solution.py
+++ b/solution.py
@@ -445,13 +445,13 @@
 def mix_y_kernel(r_ref, g_ref, o_ref):
     for k in range(r_ref.shape[0]):
         o_ref[k] = lax.dot_general(
-            r_ref[k], g_ref[...], (((0,), (0,)), ((), ())), preferred_element_type=F32
+            r_ref[k], g_ref[...], (((0,), (1,)), ((), ())), preferred_element_type=F32
         )
 
 
 def mix_y(r, g):
     groups, deep, lanes = r.shape
-    out = g.shape[1]
+    out = g.shape[0]
     take = 2 if groups % 2 == 0 else 1
     return pl.pallas_call(
         mix_y_kernel,
@@ -459,7 +459,7 @@
         out_shape=jax.ShapeDtypeStruct((groups, lanes, out), F32),
         in_specs=[
             pl.BlockSpec((take, deep, lanes), lambda i: (i, 0, 0)),
-            pl.BlockSpec((deep, out), lambda i: (0, 0)),
+            pl.BlockSpec((out, deep), lambda i: (0, 0)),
         ],
         out_specs=pl.BlockSpec((take, lanes, out), lambda i: (i, 0, 0)),
     )(r, g)
@@ -504,7 +504,7 @@
     ).astype(BF)
     r, factor_x, factor_z, factor_y = exchange(w, gt, mask, q, part_y, nx, ny, groups, span, per_c)
 
-    core = mix_y(r, gauss_kernel_north.T)
+    core = mix_y(r, gauss_kernel_north)
     core = core[:, :used].reshape(a_rows, per_c, -1).transpose(0, 2, 1)
     return (factor_x, factor_y, factor_z, core)
 

time: 122 us -> 120 us (0.984)
  local copies, waits for them, and re-layouts: 9.9 us -> 8.06 us
    unnamed x14 -> x13, local copies, waits for them, and re-layouts: 7.65 us -> 5.8 us
where the time goes in v5:
time: 120 us
  Pallas kernels  111 us (92%)
  local copies, waits for them, and re-layouts  8.06 us (7%)
    pallas_call x1, Pallas kernels, exchange(): pl.pallas_call(body, out_shape=(jax.ShapeDtypeStruct((groups, ny * span,...  70.2 us
    pallas_call x1, Pallas kernels, mix_x(): pl.pallas_call(functools.partial(mix_x_kernel, n, chunks), out_shape=(jax...  33 us
    pallas_call x1, Pallas kernels, mix_y(): pl.pallas_call(mix_y_kernel, grid=(groups // take,), out_shape=jax.ShapeD...  7.54 us
    unnamed x13, local copies, waits for them, and re-layouts  5.8 us

profile of v5, /device:TPU:1, one launch (start us, length us, event | category | flops | bytes accessed | tf_op | source)
XLA Modules:
  0.0 120.1 jit_solution(15063662282169362194)
XLA Ops:
  0.7 0.6 fusion.mask_ref
  1.3 0.0 copy-start
  1.3 1.1 tile.4
  2.4 1.2 copy.12.gt_ref
  3.5 0.0 copy-done
  3.5 1.3 %copy.18 = bf16[12,8,48,128]{3,1,2,0:T(8,128)(2,1)} copy(bf16[12,8,48,128]{3,2,1,0:T(8,128)(2,1)S(1)} %bitcast.22) | data formatting | bytes 2359296
  4.8 33.0 %shard_map.102 = (bf16[96,6144]{1,0:T(8,128)(2,1)}, f32[8,28,128]{2,1,0:T(8,128)}, f32[48,128]{1,0:T(8,128)}) custom-call(bf16[96,6144]{1,0:T(8,128)(2,1)} %bitcast.23, bf16[4,96,384]{2,1,0:T(8,128)(2,1)} %bitcast.26, bf16[96,48,128]{2,1,0:T(8,128)(2,1)} %f_ref.1, bf16[96,128]{1,0:T(8,128)(2,1)} %east_ref.1, bf16[48,128]{1,0:T(8,128)(2,1)} %north_ref.1, ...), custom_call_target="tpu_custom_call" | custom-call | tf_op jit(solution)/shard_map/pallas_call | solution.py:105
  37.8 2.6 %copy.17 = bf16[72,8,8,128]{3,1,2,0:T(8,128)(2,1)} copy(bf16[72,8,8,128]{3,2,1,0:T(8,128)(2,1)} %bitcast.25) | data formatting | bytes 2359296
  40.4 70.2 %shard_map.103 = (bf16[12,384,384]{2,1,0:T(8,128)(2,1)}, f32[96,128]{1,0:T(8,128)}, f32[128,128]{1,0:T(8,128)}, f32[48,128]{1,0:T(8,128)}) custom-call(bf16[576,1024]{1,0:T(8,128)(2,1)} %bitcast.21, bf16[8,128,384]{2,1,0:T(8,128)(2,1)} %copy.12.gt_ref, bf16[8,384]{1,0:T(8,128)(2,1)} %fusion.mask_ref, f32[8,28,128]{2,1,0:T(8,128)} %get-tuple-element.12.q_ref, ...), custom_call_target="tpu_custom_call" | custom-call | tf_op jit(solution)/shard_map/pallas_call | solution.py:430
  110.7 0.0 copy-start.2
  110.7 0.0 copy-start.3
  110.7 0.0 copy-start.1
  110.7 7.5 %shard_map.104 = f32[12,384,384]{2,1,0:T(8,128)} custom-call(bf16[12,384,384]{2,1,0:T(8,128)(2,1)} %get-tuple-element.17.r_ref, bf16[384,384]{1,0:T(8,128)(2,1)} %g_ref.1), custom_call_target="tpu_custom_call" | custom-call | tf_op jit(solution)/shard_map/pallas_call | solution.py:456
  118.2 0.0 copy-done.2
  118.2 0.6 copy.22
  118.8 0.0 copy-done.3
  118.8 0.6 copy.23
  119.5 0.0 copy-done.1
  119.5 0.6 copy.24
  (2 shorter events, 0.0 us)
Async XLA Ops:
  1.3 2.3 %copy-start = (bf16[96,48,128]{2,1,0:T(8,128)(2,1)S(1)}, bf16[96,48,128]{2,1,0:T(8,128)(2,1)}, u32[]{:S(2)}) copy-start(bf16[96,48,128]{2,1,0:T(8,128)(2,1)} %f_ref.1) | copy-start | bytes 3538948
  110.7 7.6 %copy-start.2 = (f32[96,128]{1,0:T(8,128)S(1)}, f32[96,128]{1,0:T(8,128)}, u32[]{:S(2)}) copy-start(f32[96,128]{1,0:T(8,128)} %get-tuple-element.24) | copy-start | bytes 147460
  110.7 8.2 %copy-start.3 = (f32[48,128]{1,0:T(8,128)S(1)}, f32[48,128]{1,0:T(8,128)}, u32[]{:S(2)}) copy-start(f32[48,128]{1,0:T(8,128)} %get-tuple-element.25) | copy-start | bytes 73732
  110.7 8.8 %copy-start.1 = (f32[128,128]{1,0:T(8,128)S(1)}, f32[128,128]{1,0:T(8,128)}, u32[]{:S(2)}) copy-start(f32[128,128]{1,0:T(8,128)} %get-tuple-element.26) | copy-start | bytes 196612
